TPU v7x, 512 devices: a whole 4x4x16 slice. The times are simulated.
512 devices in a mesh: net: 16 (over z), seg: 8 (over y, core), corner: 4 (over x).
Axes of the slice: x: 4, y: 4, z: 16, core: 2. Of those that a mesh axis runs over, the one named last changes fastest.
Arguments:
- tile_values: bfloat16 [8192, 128, 1024], P(('net', 'seg', 'corner')), may hold values from -48 to 48
- tile_coords: int32 [8192, 3], P(('net', 'seg', 'corner')), may hold values from 0 to 511, as said below
- tile_count: int32 [512], P(('net', 'seg', 'corner')), may hold values from 12 to 16, as said below
- owner_map: int32 [512], P('net'), may hold values from 0 to 511, as said below
- corner_factor: bfloat16 [64, 256], P('corner')
- seg_factor: bfloat16 [65536, 256], P(('seg', 'net'))
Outputs:
- net_factor: float32 [65536, 256], P(('net', 'seg', 'corner'))
Inputs may be any that keep to these rules, and one draw needn't show every extreme that they name: `tile_coords`: row t of device d gives a corner block within the corner range stored by d's corner index, a net block that owner_map assigns to an owner slot of d's net index, and a segment block within the segment range of d's seg index. Among a device's 16 rows at most 2 name segment blocks stored by any one device of the net axis, and on every device two live rows name segment blocks stored by the same device of the net axis. The first tile_count[d] rows of device d are live; the others are ignored. `owner_map`: A permutation of the 512 net blocks.
All inputs are finite; a program needn't handle non-finite values.
Results may differ from a plain program's by a relative error of at most 0.0058.
The roundings to bfloat16 on the way count: a program that leaves them out, or rounds other values in their place, can miss the bound.
Values may be sent and summed in bfloat16 or wider, within the bound.
No kernel may reach another device: no remote copies, remote signals or barrier semaphores. Data moves between devices by JAX's collectives and lax.ppermute only.
A program may use at most 64 MiB of HBM per device.

v0:
```python
import jax
import jax.numpy as jnp
from jax import lax
from jax.sharding import PartitionSpec as P

CBLK = 8
GRP = 4


def solve_rows(gram, mttkrp):
    cholesky_low = jnp.linalg.cholesky(gram)
    forward = lax.linalg.triangular_solve(cholesky_low, mttkrp.T, left_side=True, lower=True)
    backward = lax.linalg.triangular_solve(
        cholesky_low, forward, left_side=True, lower=True, transpose_a=True
    )
    return backward.T


def contract(packed):
    values, corner_rows, seg_rows = packed
    khatri = (
        corner_rows.astype(jnp.float32)[:, :, None, :] * seg_rows.astype(jnp.float32)[:, None, :, :]
    ).astype(jnp.bfloat16)
    khatri = khatri.reshape(values.shape[0], values.shape[2], corner_rows.shape[2])
    return jnp.einsum("tnj,tjr->tnr", values, khatri, preferred_element_type=jnp.float32)


def body(tile_values, tile_coords, tile_count, owner_map, corner_factor, seg_factor):
    slot_total = tile_values.shape[0]
    net_rows = tile_values.shape[1]
    columns = corner_factor.shape[1]
    seg_width = tile_values.shape[2] // CBLK
    held_blocks = seg_factor.shape[0] // seg_width
    net_devices = lax.axis_size("net")
    corner_local = tile_coords[:, 0] - lax.axis_index("corner") * (corner_factor.shape[0] // CBLK)
    seg_local = tile_coords[:, 2] - lax.axis_index("seg") * (held_blocks * net_devices)
    corner_sel = jnp.take(corner_factor.reshape(-1, CBLK, columns), corner_local, axis=0)
    gathered = lax.all_gather(seg_factor, "net", axis=0, tiled=True)
    seg_sel = jnp.take(gathered.reshape(-1, seg_width, columns), seg_local, axis=0)
    groups = slot_total // GRP
    partial_value = lax.map(
        contract,
        (
            tile_values.reshape(groups, GRP, net_rows, -1),
            corner_sel.reshape(groups, GRP, CBLK, columns),
            seg_sel.reshape(groups, GRP, seg_width, columns),
        ),
    )
    partial_value = partial_value.reshape(slot_total, net_rows * columns)
    live_mask = jnp.arange(slot_total, dtype=jnp.int32) < tile_count[0]
    member = ((tile_coords[:, 1][:, None] == owner_map[None, :]) & live_mask[:, None]).astype(
        jnp.float32
    )
    summed = jnp.dot(
        member.T, partial_value, precision=lax.Precision.HIGHEST, preferred_element_type=jnp.float32
    )
    mttkrp = lax.psum_scatter(
        summed.reshape(net_rows * lax.axis_size(("seg", "corner")), columns),
        ("seg", "corner"),
        scatter_dimension=0,
        tiled=True,
    )
    corner_part = jnp.dot(corner_factor.T, corner_factor, preferred_element_type=jnp.float32)
    seg_part = jnp.dot(seg_factor.T, seg_factor, preferred_element_type=jnp.float32)
    seg_gram = lax.psum(seg_part, ("net", "seg"))
    corner_gram = lax.psum(corner_part, "corner")
    return solve_rows(corner_gram * seg_gram, mttkrp)


def solution(mesh):
    return jax.shard_map(
        body,
        mesh=mesh,
        in_specs=(
            P(("net", "seg", "corner"), None, None),
            P(("net", "seg", "corner"), None),
            P(("net", "seg", "corner")),
            P("net"),
            P("corner", None),
            P(("seg", "net"), None),
        ),
        out_specs=P(("net", "seg", "corner"), None),
        check_vma=False,
    )
```

profile of v0, /device:TPU:8, one launch (start us, length us, event | category | flops | bytes accessed | tf_op | source)
XLA Modules:
  0.0 481.0 jit_solution(18225845388589294858)
XLA Ops:
  7.4 0.7 all-gather.2.cloned.1.call-update
  8.1 2.1 fusion.23
  10.3 1.0 fusion.22
  11.4 0.7 slice_bitcast_fusion.6
  12.1 0.8 and_reduce_fusion
  14.3 79.2 %all-gather.2.cloned.1.call-done = bf16[8192,256]{1,0:T(8,128)(2,1)} async-done(((bf16[512,256]{1,0:T(8,128)(2,1)}), bf16[8192,256]{1,0:T(8,128)(2,1)}) %all-gather.2.cloned.1.call-update) | async-done | bytes 4194320 | tf_op jit(solution)/shard_map/all_gather | solution.py:38
  93.5 2.8 gather_fusion.1
  96.5 12.6 %while.11 = (s32[]{:T(128)}, f32[4,4,128,256]{3,2,1,0:T(8,128)}, bf16[4,4,128,1024]{3,2,1,0:T(8,128)(2,1)}, bf16[4,4,8,256]{3,2,1,0:T(8,128)(2,1)S(1)}, bf16[4,4,128,256]{3,2,1,0:T(8,128)(2,1)S(1)}, /*index=5*/s32[]{:T(128)}) while((s32[]{:T(128)}, f32[4,4,128,256]{3,2,1,0:T(8,128)}, bf16[4,4,128,1024]{3,2,1,0:T(8,128)(2,1)}, ...), condition=%wide.region_7.8_spmd, body=%wide.region_6.7_spmd.sunk | while | flops 270671872 | bytes 7160917 | solution.py:41
  96.6 0.6 multiply_convert_fusion.2
  97.2 2.5 fusion.43
  100.3 2.5 fusion.43
  103.5 2.5 fusion.43
  106.6 2.5 fusion.43
  109.1 2.8 copy.13
  111.9 3.5 fusion.15
  115.5 4.9 %reshape.80 = f32[4096,256]{1,0:T(8,128)} reshape(f32[32,32768]{1,0:T(8,128)} %fusion.15) | data formatting | bytes 8388608 | tf_op jit(solution)/shard_map/reshape | solution.py:58
  120.4 232.0 %all-reduce.6.cloned.1.call-done = f32[256,256]{0,1:T(8,128)} async-done(((f32[256,256]{0,1:T(8,128)}), f32[256,256]{0,1:T(8,128)}) %all-reduce.6.cloned.1.call-update) | async-done | bytes 262160 | tf_op jit(solution)/shard_map/psum | solution.py:65
  352.4 56.2 %all-reduce.4.cloned.1.call-done = f32[256,256]{0,1:T(8,128)} async-done(((f32[256,256]{0,1:T(8,128)}), f32[256,256]{0,1:T(8,128)}) %all-reduce.4.cloned.1.call-update) | async-done | bytes 262160 | tf_op jit(solution)/shard_map/psum | solution.py:66
  408.6 1.1 mul.24
  409.8 11.7 %cholesky.50 = f32[128,128]{1,0:T(8,128)S(1)} custom-call(f32[128,128]{1,0:T(8,128)S(1)} %cholesky.118), custom_call_target="Cholesky" | custom-call | tf_op jit(solution)/shard_map/jit(cholesky)/cholesky | solution.py:11
  421.6 9.8 %custom-call.16 = f32[1,128,128]{1,2,0:T(8,128)S(1)} custom-call(f32[1,128,128]{2,1,0:T(8,128)S(1)} %get-tuple-element.68), custom_call_target="InvertDiagBlocksLowerTriangular" | custom-call | tf_op jit(solution)/shard_map/jit(cholesky)/cholesky | solution.py:11
  431.9 11.7 %cholesky.105 = f32[128,128]{1,0:T(8,128)S(1)} custom-call(f32[128,128]{1,0:T(8,128)S(1)} %convolution_subtract_fusion.2), custom_call_target="Cholesky" | custom-call | tf_op jit(solution)/shard_map/jit(cholesky)/cholesky | solution.py:11
  443.7 0.7 compare_reduce_fusion
  445.7 3.9 while.12
  445.7 0.6 fusion.44
  446.3 1.3 bitcast_dynamic-update-slice_fusion.2
  447.7 0.6 fusion.44
  448.3 1.3 bitcast_dynamic-update-slice_fusion.2
  449.6 19.9 %custom-call.17 = f32[2,128,128]{1,2,0:T(8,128)S(1)} custom-call(f32[2,128,128]{2,1,0:T(8,128)S(1)} %get-tuple-element.40), custom_call_target="InvertDiagBlocksLowerTriangular" | custom-call | tf_op jit(solution)/shard_map/triangular_solve | solution.py:13
  469.5 1.1 fusion.5
  470.7 1.1 convolution_subtract_fusion.1
  472.8 0.8 copy.10
  (51 shorter events, 5.0 us)
Async XLA Ops:
  7.4 2.9 copy-start
  7.4 86.2 %all-gather.2.cloned.1.call-start = ((), (), s32[]{:S(2)}) async-start(), calls=%async_computation.3 | async-start | bytes 4456448 | tf_op jit(solution)/shard_map/all_gather | solution.py:38
  8.1 344.3 %all-reduce.6.cloned.1.call-start = ((), (), s32[]{:S(2)}) async-start(), calls=%async_computation.2 | async-start | bytes 524288 | tf_op jit(solution)/shard_map/psum | solution.py:65
  10.3 398.3 %all-reduce.4.cloned.1.call-start = ((), (), s32[]{:S(2)}) async-start(), calls=%async_computation.1 | async-start | bytes 524288 | tf_op jit(solution)/shard_map/psum | solution.py:66
  11.3 458.2 %reduce-scatter.2.cloned.1.call-start = ((), (), s32[]{:S(2)}) async-start(), calls=%async_computation.4 | async-start | bytes 4325376 | tf_op jit(solution)/shard_map/reduce_scatter | solution.py:57
  109.1 2.8 copy-start.1
Sparse Core Ops, SparseCore 0:
  10.3 83.2 all-gather.1
  120.5 101.2 reduce-scatter.1
Sparse Core Ops, SparseCore 1:
  12.4 339.9 all-reduce.5
  354.7 53.8 all-reduce.3
where the time goes:
time: 482 us; the launch traced here: 481 us
  waiting for transfers between devices  368 us (76%)
  other arithmetic  58.6 us (12%)
  matrix products  20.2 us (4%)
  between operations  17 us (4%)
  local copies, waits for them, and re-layouts  16.8 us (3%)
    psum x1, waiting for transfers between devices, body(): seg_gram = lax.psum(seg_part, ('net', 'seg'))  232 us
    all_gather x1, waiting for transfers between devices, body(): gathered = lax.all_gather(seg_factor, 'net', axis=0, tiled=True)  79.2 us
    psum x1, waiting for transfers between devices, body(): corner_gram = lax.psum(corner_part, 'corner')  56.2 us
    another operation x6, other arithmetic, solve_rows(): cholesky_low = jnp.linalg.cholesky(gram)  34 us
    another operation x3, other arithmetic, solve_rows(): lax.linalg.triangular_solve(cholesky_low, forward, left_side=True, lower=...  19.9 us
    dot_general x4, matrix products, contract(): jnp.einsum('tnj,tjr->tnr', values, khatri, preferred_element_type=jnp.flo...  9.96 us
  transfers between devices with their start and end apart: 4, of which 3 were waited for; matrix products, arithmetic and copies ran while one was open for 19% of the time, Pallas kernels for 0%

commit v1 on v0

--- a/solution.py
+++ b/solution.py
@@ -1,3 +1,4 @@
+import functools
 import jax
 import jax.numpy as jnp
 from jax import lax
@@ -5,6 +6,18 @@
 
 CBLK = 8
 GRP = 4
+
+
+def _clear_cells(x_part, comm_axis):
+    workers = jax.lax.axis_size(comm_axis)
+    upper = lambda high: [(ix, ix ^ high) for ix in range(workers)]
+    later = x_part
+    for dev in range(workers.bit_length() - 1):
+        later = later + jax.lax.ppermute(later, comm_axis, upper(1 << dev))
+    return later
+
+
+raise_matrix = functools.partial(_clear_cells, comm_axis="corner")
 
 
 def solve_rows(gram, mttkrp):
@@ -63,7 +76,7 @@
     corner_part = jnp.dot(corner_factor.T, corner_factor, preferred_element_type=jnp.float32)
     seg_part = jnp.dot(seg_factor.T, seg_factor, preferred_element_type=jnp.float32)
     seg_gram = lax.psum(seg_part, ("net", "seg"))
-    corner_gram = lax.psum(corner_part, "corner")
+    corner_gram = raise_matrix(corner_part)
     return solve_rows(corner_gram * seg_gram, mttkrp)
 
 

time: 482 us -> 426 us (0.88)
  the two profiles are of different devices: /device:TPU:8 before, /device:TPU:1 now
where the time goes in v1:
time: 426 us; the launch traced here: 425 us
  waiting for transfers between devices  305 us (72%)
  other arithmetic  58.3 us (14%)
  matrix products  19.5 us (5%)
  between operations  17 us (4%)
  local copies, waits for them, and re-layouts  16.8 us (4%)
  starting transfers between devices  8.11 us (2%)
    psum x1, waiting for transfers between devices, body(): seg_gram = lax.psum(seg_part, ('net', 'seg'))  227 us
    all_gather x1, waiting for transfers between devices, body(): gathered = lax.all_gather(seg_factor, 'net', axis=0, tiled=True)  73 us
    another operation x6, other arithmetic, solve_rows(): cholesky_low = jnp.linalg.cholesky(gram)  34 us
    another operation x3, other arithmetic, solve_rows(): lax.linalg.triangular_solve(cholesky_low, forward, left_side=True, lower=...  19.7 us
    dot_general x4, matrix products, contract(): jnp.einsum('tnj,tjr->tnr', values, khatri, preferred_element_type=jnp.flo...  9.96 us
  transfers between devices with their start and end apart: 5, of which 3 were waited for; matrix products, arithmetic and copies ran while one was open for 21% of the time, Pallas kernels for 0%

profile of v1, /device:TPU:1, one launch (start us, length us, event | category | flops | bytes accessed | tf_op | source)
XLA Modules:
  0.0 425.0 jit_solution(18317328971682359909)
XLA Ops:
  7.4 0.7 all-gather.2.cloned.1.call-update
  8.1 2.1 fusion.23
  10.3 0.7 slice_bitcast_fusion.6
  11.0 0.8 and_reduce_fusion
  13.3 73.0 %all-gather.2.cloned.1.call-done = bf16[8192,256]{1,0:T(8,128)(2,1)} async-done(((bf16[512,256]{1,0:T(8,128)(2,1)}), bf16[8192,256]{1,0:T(8,128)(2,1)}) %all-gather.2.cloned.1.call-update) | async-done | bytes 4194320 | tf_op jit(solution)/shard_map/all_gather | solution.py:51
  86.3 2.8 gather_fusion.1
  89.3 12.6 %while.11 = (s32[]{:T(128)}, f32[4,4,128,256]{3,2,1,0:T(8,128)}, bf16[4,4,128,1024]{3,2,1,0:T(8,128)(2,1)}, bf16[4,4,8,256]{3,2,1,0:T(8,128)(2,1)S(1)}, bf16[4,4,128,256]{3,2,1,0:T(8,128)(2,1)S(1)}, /*index=5*/s32[]{:T(128)}) while((s32[]{:T(128)}, f32[4,4,128,256]{3,2,1,0:T(8,128)}, bf16[4,4,128,1024]{3,2,1,0:T(8,128)(2,1)}, ...), condition=%wide.region_6.7_spmd, body=%wide.region_5.6_spmd.sunk | while | flops 270671872 | bytes 7160917 | solution.py:54
  89.9 2.5 fusion.43
  93.1 2.5 fusion.43
  96.2 2.5 fusion.43
  99.3 2.5 fusion.43
  101.8 2.8 copy.14
  104.7 3.5 fusion.15
  108.2 4.9 %reshape.80 = f32[4096,256]{1,0:T(8,128)} reshape(f32[32,32768]{1,0:T(8,128)} %fusion.15) | data formatting | bytes 8388608 | tf_op jit(solution)/shard_map/reshape | solution.py:71
  113.4 3.2 collective-permute-start
  116.5 4.3 %collective-permute-done = f32[256,256]{0,1:T(8,128)S(1)} collective-permute-done((f32[256,256]{0,1:T(8,128)S(1)}, f32[256,256]{0,1:T(8,128)S(1)}, u32[]{:S(2)}, u32[]{:S(2)}) %collective-permute-start) | collective-permute-done | bytes 262176 | tf_op jit(solution)/shard_map/ppermute | solution.py:16
  120.9 4.9 %collective-permute-start.1 = (f32[256,256]{0,1:T(8,128)S(1)}, f32[256,256]{0,1:T(8,128)S(1)}, u32[]{:S(2)}, u32[]{:S(2)}) collective-permute-start(f32[256,256]{0,1:T(8,128)S(1)} %add.49), channel_id=1, source_target_pairs={{0,2},{1,3},{2,0},{3,1},{4,6},{5,7},{6,4},{7,5},{8,10},{9,11},{10,... | collective-permute-start | bytes 786440 | tf_op jit(solution)/shard_map/ppermute | solution.py:16
  125.8 226.8 %all-reduce.3.cloned.1.call-done = f32[256,256]{0,1:T(8,128)} async-done(((f32[256,256]{0,1:T(8,128)}), f32[256,256]{0,1:T(8,128)}) %all-reduce.3.cloned.1.call-update) | async-done | bytes 262160 | tf_op jit(solution)/shard_map/psum | solution.py:78
  352.6 1.0 add_multiply_fusion
  353.8 11.7 %cholesky.50 = f32[128,128]{1,0:T(8,128)S(1)} custom-call(f32[128,128]{1,0:T(8,128)S(1)} %cholesky.118), custom_call_target="Cholesky" | custom-call | tf_op jit(solution)/shard_map/jit(cholesky)/cholesky | solution.py:24
  365.6 9.8 %custom-call.16 = f32[1,128,128]{1,2,0:T(8,128)S(1)} custom-call(f32[1,128,128]{2,1,0:T(8,128)S(1)} %get-tuple-element.68), custom_call_target="InvertDiagBlocksLowerTriangular" | custom-call | tf_op jit(solution)/shard_map/jit(cholesky)/cholesky | solution.py:24
  375.9 11.7 %cholesky.105 = f32[128,128]{1,0:T(8,128)S(1)} custom-call(f32[128,128]{1,0:T(8,128)S(1)} %convolution_subtract_fusion.2), custom_call_target="Cholesky" | custom-call | tf_op jit(solution)/shard_map/jit(cholesky)/cholesky | solution.py:24
  387.7 0.7 compare_reduce_fusion
  389.7 4.1 while.12
  389.9 0.6 fusion.44
  390.5 1.3 bitcast_dynamic-update-slice_fusion.2
  391.8 0.6 fusion.44
  392.4 1.3 bitcast_dynamic-update-slice_fusion.2
  393.8 19.7 %custom-call.17 = f32[2,128,128]{1,2,0:T(8,128)S(1)} custom-call(f32[2,128,128]{2,1,0:T(8,128)S(1)} %get-tuple-element.40), custom_call_target="InvertDiagBlocksLowerTriangular" | custom-call | tf_op jit(solution)/shard_map/triangular_solve | solution.py:26
  413.5 1.1 fusion.5
  414.6 1.1 convolution_subtract_fusion.1
  416.8 0.8 copy.11
  (53 shorter events, 5.7 us)
Async XLA Ops:
  7.4 5.3 %copy-start = (bf16[16,256]{1,0:T(8,128)(2,1)S(1)}, bf16[16,256]{1,0:T(8,128)(2,1)}, u32[]{:S(2)}) copy-start(bf16[16,256]{1,0:T(8,128)(2,1)} %param.12) | copy-start | bytes 24580
  7.4 78.9 %all-gather.2.cloned.1.call-start = ((), (), s32[]{:S(2)}) async-start(), calls=%async_computation.2 | async-start | bytes 4456448 | tf_op jit(solution)/shard_map/all_gather | solution.py:51
  8.1 344.5 %all-reduce.3.cloned.1.call-start = ((), (), s32[]{:S(2)}) async-start(), calls=%async_computation.1 | async-start | bytes 524288 | tf_op jit(solution)/shard_map/psum | solution.py:78
  10.2 403.2 %reduce-scatter.2.cloned.1.call-start = ((), (), s32[]{:S(2)}) async-start(), calls=%async_computation.3 | async-start | bytes 4325376 | tf_op jit(solution)/shard_map/reduce_scatter | solution.py:70
  101.8 2.8 copy-start.1
  113.4 7.5 %collective-permute-start = (f32[256,256]{0,1:T(8,128)S(1)}, f32[256,256]{0,1:T(8,128)S(1)}, u32[]{:S(2)}, u32[]{:S(2)}) collective-permute-start(f32[256,256]{0,1:T(8,128)S(1)} %fusion.22), channel_id=1, source_target_pairs={{0,1},{1,0},{2,3},{3,2},{4,5},{5,4},{6,7},{7,6},{8,9},{9,8},{10,11... | collective-permute-start | bytes 786440 | tf_op jit(solution)/shard_map/ppermute | solution.py:16
  120.9 231.7 %collective-permute-start.1 = (f32[256,256]{0,1:T(8,128)S(1)}, f32[256,256]{0,1:T(8,128)S(1)}, u32[]{:S(2)}, u32[]{:S(2)}) collective-permute-start(f32[256,256]{0,1:T(8,128)S(1)} %add.49), channel_id=1, source_target_pairs={{0,2},{1,3},{2,0},{3,1},{4,6},{5,7},{6,4},{7,5},{8,10},{9,11},{10,... | collective-permute-start | bytes 786440 | tf_op jit(solution)/shard_map/ppermute | solution.py:16
Sparse Core Ops, SparseCore 0:
  10.3 75.9 all-gather.1
  113.2 108.0 reduce-scatter.1
Sparse Core Ops, SparseCore 1:
  12.4 340.1 all-reduce.2

commit v2 on v0

--- a/solution.py
+++ b/solution.py
@@ -35,7 +35,9 @@
     corner_local = tile_coords[:, 0] - lax.axis_index("corner") * (corner_factor.shape[0] // CBLK)
     seg_local = tile_coords[:, 2] - lax.axis_index("seg") * (held_blocks * net_devices)
     corner_sel = jnp.take(corner_factor.reshape(-1, CBLK, columns), corner_local, axis=0)
-    gathered = lax.all_gather(seg_factor, "net", axis=0, tiled=True)
+    found_now = jnp.stack([seg_factor for _ in range(lax.axis_size("net"))])
+    newest = lax.all_to_all(found_now, "net", 0, 0)
+    gathered = jnp.concatenate(newest, axis=0)
     seg_sel = jnp.take(gathered.reshape(-1, seg_width, columns), seg_local, axis=0)
     groups = slot_total // GRP
     partial_value = lax.map(

time: 482 us -> 559 us (1.16)
  waiting for transfers between devices: 368 us -> 429 us
  starting transfers between devices: 0.13 us -> 15.5 us
    all_to_all x0 -> x1, waiting for transfers between devices: none -> 180 us  [body(): newest = lax.all_to_all(found_now, 'net', 0, 0)]
    all_gather x1 -> x0, waiting for transfers between devices: 79.2 us -> none  [body(): gathered = lax.all_gather(seg_factor, 'net', axis=0, tiled=True)]
    psum x1, waiting for transfers between devices: 232 us -> 193 us  [body(): seg_gram = lax.psum(seg_part, ('net', 'seg'))]
    all_to_all x0 -> x1, starting transfers between devices: none -> 15.4 us  [body(): newest = lax.all_to_all(found_now, 'net', 0, 0)]
  transfers between devices with their start and end apart: 4 -> 4, of which waited for: 3 -> 3; matrix products, arithmetic and copies ran while one was open for 19% -> 16% of each run, Pallas kernels for 0% -> 0%
where the time goes in v2:
time: 559 us
  waiting for transfers between devices  429 us (77%)
  other arithmetic  57.8 us (10%)
  local copies, waits for them, and re-layouts  19.4 us (3%)
  matrix products  19.2 us (3%)
  between operations  17 us (3%)
  starting transfers between devices  15.5 us (3%)
    psum x1, waiting for transfers between devices, body(): seg_gram = lax.psum(seg_part, ('net', 'seg'))  193 us
    all_to_all x1, waiting for transfers between devices, body(): newest = lax.all_to_all(found_now, 'net', 0, 0)  180 us
    psum x1, waiting for transfers between devices, body(): corner_gram = lax.psum(corner_part, 'corner')  56.5 us
    another operation x6, other arithmetic, solve_rows(): cholesky_low = jnp.linalg.cholesky(gram)  34 us
    another operation x3, other arithmetic, solve_rows(): lax.linalg.triangular_solve(cholesky_low, forward, left_side=True, lower=...  19.9 us
    all_to_all x1, starting transfers between devices, body(): newest = lax.all_to_all(found_now, 'net', 0, 0)  15.4 us
  transfers between devices with their start and end apart: 4, of which 3 were waited for; matrix products, arithmetic and copies ran while one was open for 16% of the time, Pallas kernels for 0%

profile of v2, /device:TPU:8, one launch (start us, length us, event | category | flops | bytes accessed | tf_op | source)
XLA Modules:
  0.0 558.6 jit_solution(3753553670603413467)
XLA Ops:
  7.4 3.3 stack.2
  10.7 15.4 %all-to-all-start = ((bf16[16,512,256]{2,1,0:T(8,128)(2,1)}), bf16[16,512,256]{2,1,0:T(8,128)(2,1)}, u32[]{:S(2)}, u32[]{:S(2)}) async-start(bf16[16,512,256]{2,1,0:T(8,128)(2,1)} %stack.2), calls=%async_computation | async-start | bytes 8388608 | tf_op jit(solution)/shard_map/all_to_all | solution.py:39
  26.2 1.0 fusion.23
  27.2 0.9 fusion.22
  29.8 179.9 %all-to-all-done = bf16[16,512,256]{2,1,0:T(8,128)(2,1)} async-done(((bf16[16,512,256]{2,1,0:T(8,128)(2,1)}), bf16[16,512,256]{2,1,0:T(8,128)(2,1)}, u32[]{:S(2)}, u32[]{:S(2)}) %all-to-all-start) | async-done | bytes 4194336 | tf_op jit(solution)/shard_map/all_to_all | solution.py:39
  209.7 2.8 gather_fusion.1
  212.7 12.6 %while.11 = (s32[]{:T(128)}, f32[4,4,128,256]{3,2,1,0:T(8,128)}, bf16[4,4,128,1024]{3,2,1,0:T(8,128)(2,1)}, bf16[4,4,8,256]{3,2,1,0:T(8,128)(2,1)S(1)}, bf16[4,4,128,256]{3,2,1,0:T(8,128)(2,1)S(1)}, /*index=5*/s32[]{:T(128)}) while((s32[]{:T(128)}, f32[4,4,128,256]{3,2,1,0:T(8,128)}, bf16[4,4,128,1024]{3,2,1,0:T(8,128)(2,1)}, ...), condition=%wide.region_7.8_spmd, body=%wide.region_6.7_spmd.sunk | while | flops 270671872 | bytes 7160909 | solution.py:43
  213.4 2.5 fusion.43
  216.0 0.6 multiply_convert_fusion.2
  216.6 2.5 fusion.43
  219.2 0.6 multiply_convert_fusion.2
  219.7 2.5 fusion.43
  222.9 2.5 fusion.43
  225.3 2.8 copy.13
  228.2 3.5 fusion.15
  231.7 4.9 reshape.78
  236.6 193.0 %all-reduce.6.cloned.1.call-done = f32[256,256]{0,1:T(8,128)} async-done(((f32[256,256]{0,1:T(8,128)}), f32[256,256]{0,1:T(8,128)}) %all-reduce.6.cloned.1.call-update) | async-done | bytes 262160 | tf_op jit(solution)/shard_map/psum | solution.py:67
  429.6 56.5 %all-reduce.4.cloned.1.call-done = f32[256,256]{0,1:T(8,128)} async-done(((f32[256,256]{0,1:T(8,128)}), f32[256,256]{0,1:T(8,128)}) %all-reduce.4.cloned.1.call-update) | async-done | bytes 262160 | tf_op jit(solution)/shard_map/psum | solution.py:68
  486.1 1.1 mul.24
  487.4 11.7 %cholesky.50 = f32[128,128]{1,0:T(8,128)S(1)} custom-call(f32[128,128]{1,0:T(8,128)S(1)} %cholesky.118), custom_call_target="Cholesky" | custom-call | tf_op jit(solution)/shard_map/jit(cholesky)/cholesky | solution.py:11
  499.1 9.8 %custom-call.16 = f32[1,128,128]{1,2,0:T(8,128)S(1)} custom-call(f32[1,128,128]{2,1,0:T(8,128)S(1)} %get-tuple-element.68), custom_call_target="InvertDiagBlocksLowerTriangular" | custom-call | tf_op jit(solution)/shard_map/jit(cholesky)/cholesky | solution.py:11
  509.5 11.7 %cholesky.105 = f32[128,128]{1,0:T(8,128)S(1)} custom-call(f32[128,128]{1,0:T(8,128)S(1)} %convolution_subtract_fusion.2), custom_call_target="Cholesky" | custom-call | tf_op jit(solution)/shard_map/jit(cholesky)/cholesky | solution.py:11
  521.2 0.7 compare_reduce_fusion
  523.2 3.9 while.12
  523.2 0.6 fusion.44
  523.9 1.3 bitcast_dynamic-update-slice_fusion.2
  525.2 0.6 fusion.44
  525.8 1.3 bitcast_dynamic-update-slice_fusion.2
  527.1 19.9 %custom-call.17 = f32[2,128,128]{1,2,0:T(8,128)S(1)} custom-call(f32[2,128,128]{2,1,0:T(8,128)S(1)} %get-tuple-element.40), custom_call_target="InvertDiagBlocksLowerTriangular" | custom-call | tf_op jit(solution)/shard_map/triangular_solve | solution.py:13
  547.1 1.1 fusion.5
  548.2 1.1 convolution_subtract_fusion.1
  550.4 0.8 copy.10
  (55 shorter events, 4.4 us)
Async XLA Ops:
  7.4 19.9 %copy-start = (bf16[16,256]{1,0:T(8,128)(2,1)S(1)}, bf16[16,256]{1,0:T(8,128)(2,1)}, u32[]{:S(2)}) copy-start(bf16[16,256]{1,0:T(8,128)(2,1)} %param.12) | copy-start | bytes 24580
  10.7 15.4 %copy-start.1 = (bf16[512,256]{1,0:T(8,128)(2,1)S(1)}, bf16[512,256]{1,0:T(8,128)(2,1)}, u32[]{:S(2)}) copy-start(bf16[512,256]{1,0:T(8,128)(2,1)} %param.13) | copy-start | bytes 786436
  10.7 17.5 %copy-start.3 = (s32[16,3]{0,1:T(4,128)S(1)}, s32[16,3]{0,1:T(4,128)}, u32[]{:S(2)}) copy-start(s32[16,3]{0,1:T(4,128)} %param.9) | copy-start | bytes 580
  10.7 199.0 %all-to-all-start = ((bf16[16,512,256]{2,1,0:T(8,128)(2,1)}), bf16[16,512,256]{2,1,0:T(8,128)(2,1)}, u32[]{:S(2)}, u32[]{:S(2)}) async-start(bf16[16,512,256]{2,1,0:T(8,128)(2,1)} %stack.2), calls=%async_computation | async-start | bytes 8388608 | tf_op jit(solution)/shard_map/all_to_all | solution.py:39
  26.1 403.5 %all-reduce.6.cloned.1.call-start = ((), (), s32[]{:S(2)}) async-start(), calls=%async_computation.3 | async-start | bytes 524288 | tf_op jit(solution)/shard_map/psum | solution.py:67
  27.2 459.0 %all-reduce.4.cloned.1.call-start = ((), (), s32[]{:S(2)}) async-start(), calls=%async_computation.2 | async-start | bytes 524288 | tf_op jit(solution)/shard_map/psum | solution.py:68
  28.2 518.9 %reduce-scatter.2.cloned.1.call-start = ((), (), s32[]{:S(2)}) async-start(), calls=%async_computation.4 | async-start | bytes 4325376 | tf_op jit(solution)/shard_map/reduce_scatter | solution.py:59
  225.3 2.8 copy-start.2
Sparse Core Ops, SparseCore 0:
  30.8 398.8 all-reduce.5
  432.1 54.0 all-reduce.3
Sparse Core Ops, SparseCore 1:
  236.7 104.5 reduce-scatter.1
